TPU v7x, 32 devices: a whole 2x2x4 slice. The times are simulated.
32 devices in a mesh: dp: 8 (over z, y), section: 2 (over core), tensor: 2 (over x).
Axes of the slice: x: 2, y: 2, z: 4, core: 2. Of those that a mesh axis runs over, the one named last changes fastest.
Arguments:
- tokens: bfloat16 [128, 32, 1024], P('dp'), may hold values from -6 to 6
- counts: int32 [128], replicated, may hold values from 8 to 32, as said below
- assign: int32 [128], replicated, may hold values from 0 to 127, as said below
- qkv_weight: bfloat16 [2, 1024, 3, 1024], P('section', 'dp', None, 'tensor'), may hold values from -0.9375 to 0.9375
- out_weight: bfloat16 [2, 1024, 1024], P('section', 'dp'), may hold values from -0.1875 to 0.1875
- up_weight: bfloat16 [2, 1024, 4096], P('section', 'dp', 'tensor'), may hold values from -0.1875 to 0.1875
- up_bias: bfloat16 [2, 4096], P('section', 'tensor'), may hold values from -3 to 3
- down_weight: bfloat16 [2, 4096, 1024], P('section', 'tensor', 'dp'), may hold values from -0.09375 to 0.09375
- attn_gain: bfloat16 [2, 1024], P('section'), may hold values from 0.25 to 1.75
- mlp_gain: bfloat16 [2, 1024], P('section'), may hold values from 0.25 to 1.75
- final_gain: bfloat16 [1024], replicated, may hold values from 0.25 to 1.75
Outputs:
- encoded: bfloat16 [128, 32, 1024], P('dp', 'section', 'tensor')
Inputs may be any that keep to these rules, and one draw needn't show every extreme that they name: `counts`: every count is at least 8, and in every draw some image has all 32 slots live. assign is a permutation of the images. Slot j belongs to data group j // 16, so every data group receives 16 images; within one data group's slots the images stand in increasing order. Images of data group g are tokens rows g * 16 to (g + 1) * 16 - 1. No data group hands more than 2 images to one data group (itself included), and in every draw some pair of data groups exchanges exactly 2. Every data group receives some image from the data group half the axis away.
All inputs are finite; a program needn't handle non-finite values.
Results may differ from a plain program's by a relative error of at most 0.024.
The roundings to bfloat16 on the way count: a program that leaves them out, or rounds other values in their place, can miss the bound.
Values may be sent and summed in bfloat16 or wider, within the bound.
A program may use at most 128 MiB of HBM per device.

v0:
```python
import jax
import jax.numpy as jnp
from jax import lax
from jax.sharding import PartitionSpec as P

MICRO = 4
HEAD_DIM = 64


epsilon = 1e-06


def passed_along(value, axis, by):
    size = lax.axis_size(axis)
    return lax.ppermute(value, axis, [(i, (i + by) % size) for i in range(size)])


def broadcast(value, axis, root):
    mine = lax.axis_index(axis) == root
    return lax.psum(jnp.where(mine, value, jnp.zeros_like(value)), axis)


def layer_norm(values, gain_vector):
    average = jnp.mean(values, axis=-1, keepdims=True)
    centred = values - average
    spread = jnp.mean(centred * centred, axis=-1, keepdims=True)
    return centred * lax.rsqrt(spread + epsilon) * gain_vector.astype(jnp.float32)


def attend(normed, w_merged, live_count, head_dim):
    row_count = normed.shape[0]
    merged = jnp.dot(
        normed, w_merged.reshape(w_merged.shape[0], -1), preferred_element_type=jnp.float32
    )
    merged = merged.reshape(row_count, 3, -1, head_dim)
    scores = jnp.einsum(
        "qhd,khd->hqk", merged[:, 0], merged[:, 1], precision=lax.Precision.HIGHEST
    ) * head_dim ** (-0.5)
    visible = jnp.arange(row_count) < live_count
    scores = jnp.where(visible[None, None, :], scores, -1e30)
    weights = jax.nn.softmax(scores, axis=-1)
    mixed = jnp.einsum("hqk,khd->qhd", weights, merged[:, 2], precision=lax.Precision.HIGHEST)
    return mixed.reshape(row_count, -1).astype(jnp.bfloat16)


def local(
    tokens,
    counts,
    assign,
    qkv_weight,
    out_weight,
    up_weight,
    up_bias,
    down_weight,
    attn_gain,
    mlp_gain,
    final_gain,
):
    groups = lax.axis_size("dp")
    sections = lax.axis_size("section")
    tensor_ranks = lax.axis_size("tensor")
    images_dev, block_rows, model_width = tokens.shape
    quarter = model_width // tensor_ranks
    capacity = (images_dev + groups - 1) // groups
    total_images = assign.shape[0]
    batch_images = MICRO
    batch_count = images_dev // batch_images
    my_group = lax.axis_index("dp")
    my_section = lax.axis_index("section")
    tensor_index = lax.axis_index("tensor")
    numbers = jnp.arange(total_images, dtype=jnp.int32)
    matches = (assign[:, None] == numbers[None, :]).astype(jnp.int32)
    slot_of = jnp.sum(matches * numbers[:, None], axis=0)
    target = slot_of // images_dev
    source_group = numbers // images_dev
    earlier = (
        (source_group[:, None] == source_group[None, :])
        & (target[:, None] == target[None, :])
        & (numbers[None, :] < numbers[:, None])
    )
    rank_all = jnp.sum(earlier.astype(jnp.int32), axis=1)
    send_slot = lax.dynamic_slice_in_dim(
        target * capacity + rank_all, my_group * images_dev, images_dev
    )
    buffer_slots = jnp.arange(groups * capacity, dtype=jnp.int32)
    selector = (buffer_slots[:, None] == send_slot[None, :]).astype(jnp.bfloat16)
    outgoing = jnp.einsum(
        "sl,lbd->sbd", selector, tokens, preferred_element_type=jnp.float32
    ).astype(jnp.bfloat16)
    received = lax.all_to_all(outgoing, "dp", split_axis=0, concat_axis=0, tiled=True)
    my_images = lax.dynamic_slice_in_dim(assign, my_group * images_dev, images_dev)
    chosen = (my_images[:, None] == numbers[None, :]).astype(jnp.int32)
    receive_slot = jnp.sum(chosen * (source_group * capacity + rank_all)[None, :], axis=1)
    live_counts = jnp.sum(chosen * counts[None, :], axis=1)
    picker = (buffer_slots[None, :] == receive_slot[:, None]).astype(jnp.bfloat16)
    arrived = jnp.einsum(
        "js,sbd->jbd", picker, received, preferred_element_type=jnp.float32
    ).astype(jnp.bfloat16)
    arrived_batches = arrived.reshape(batch_count, batch_images, block_rows, model_width)
    live_batches = live_counts.reshape(batch_count, batch_images)
    qkv_full, out_full, up_full, down_full = (
        lax.all_gather(qkv_weight, "dp", axis=1, tiled=True),
        lax.all_gather(out_weight, "dp", axis=1, tiled=True),
        lax.all_gather(up_weight, "dp", axis=1, tiled=True),
        lax.all_gather(down_weight, "dp", axis=2, tiled=True),
    )
    qkv_full = qkv_full[0]
    out_full = out_full[0]
    up_full = up_full[0]
    down_full = down_full[0]
    bias_row = up_bias[0].astype(jnp.float32)
    gain_attn = attn_gain[0]
    gain_mlp = mlp_gain[0]
    row_numbers = jnp.arange(block_rows)
    flat_rows = batch_images * block_rows

    def advance(step_index, state):
        carried, stored = state
        current = lax.all_gather(carried, "tensor", axis=2, tiled=True)
        done_index = step_index - sections
        finishing = (my_section == 0) & (done_index >= 0)
        done_slot = jnp.clip(done_index, 0, batch_count - 1)
        finished_rows = row_numbers[None, :, None] < live_batches[done_slot][:, None, None]
        finished = jnp.where(
            finished_rows, layer_norm(current.astype(jnp.float32), final_gain), 0.0
        ).astype(jnp.bfloat16)
        stored = jnp.where(
            finishing, lax.dynamic_update_index_in_dim(stored, finished, done_slot, 0), stored
        )
        micro_index = step_index - my_section
        active = (micro_index >= 0) & (micro_index < batch_count)
        slot_index = jnp.clip(micro_index, 0, batch_count - 1)
        injected = lax.dynamic_index_in_dim(
            arrived_batches, jnp.clip(step_index, 0, batch_count - 1), 0, keepdims=False
        )
        incoming = jnp.where(my_section == 0, injected, current)
        live_now = live_batches[slot_index]

        def attention_part():
            normed = layer_norm(incoming.astype(jnp.float32), gain_attn).astype(jnp.bfloat16)
            return jax.vmap(
                lambda image_rows, live_count: attend(image_rows, qkv_full, live_count, HEAD_DIM)
            )(normed, live_now)

        def attention_spare():
            return jnp.zeros((batch_images, block_rows, quarter), jnp.bfloat16)

        head_out = lax.cond(active, attention_part, attention_spare)
        joined = lax.all_gather(head_out, "tensor", axis=2, tiled=True)

        def mlp_part():
            middle = incoming.reshape(flat_rows, model_width).astype(jnp.float32) + jnp.dot(
                joined.reshape(flat_rows, model_width), out_full, preferred_element_type=jnp.float32
            )
            normed_mlp = layer_norm(middle, gain_mlp).astype(jnp.bfloat16)
            hidden = jax.nn.gelu(
                jnp.dot(normed_mlp, up_full, preferred_element_type=jnp.float32) + bias_row,
                approximate=False,
            ).astype(jnp.bfloat16)
            return (middle, jnp.dot(hidden, down_full, preferred_element_type=jnp.float32))

        def mlp_spare():
            empty = jnp.zeros((flat_rows, model_width), jnp.float32)
            return (empty, empty)

        middle, partial_value = lax.cond(active, mlp_part, mlp_spare)
        shares = lax.psum_scatter(
            partial_value.astype(jnp.bfloat16), "tensor", scatter_dimension=1, tiled=True
        ).astype(jnp.float32)
        own_share = lax.dynamic_slice_in_dim(middle, tensor_index * quarter, quarter, 1)
        updated = (
            (own_share + shares).astype(jnp.bfloat16).reshape(batch_images, block_rows, quarter)
        )
        carried = passed_along(updated, "section", 1)
        return (carried, stored)

    initial = (
        jnp.zeros((batch_images, block_rows, quarter), jnp.bfloat16),
        jnp.zeros((batch_count, batch_images, block_rows, model_width), jnp.bfloat16),
    )
    carried, stored = lax.fori_loop(0, batch_count + sections, advance, initial)
    stored = stored.reshape(images_dev, block_rows, model_width)
    my_piece = lax.dynamic_slice_in_dim(stored, tensor_index * quarter, quarter, 2)
    spread = broadcast(my_piece, "section", 0)
    section_rows = block_rows // sections
    return lax.dynamic_slice_in_dim(spread, my_section * section_rows, section_rows, 1)


def solution(mesh):
    in_specs = (
        P("dp", None, None),
        P(),
        P(),
        P("section", "dp", None, "tensor"),
        P("section", "dp", None),
        P("section", "dp", "tensor"),
        P("section", "tensor"),
        P("section", "tensor", "dp"),
        P("section", None),
        P("section", None),
        P(),
    )
    out_specs = P("dp", "section", "tensor")
    return jax.shard_map(local, mesh=mesh, in_specs=in_specs, out_specs=out_specs, check_vma=False)
```

profile of v0, /device:TPU:0, one launch (start us, length us, event | category | flops | bytes accessed | tf_op | source)
XLA Modules:
  0.0 576.1 jit_solution(2311422766453699122)
XLA Ops:
  14.1 7.3 %all-to-all-start = ((bf16[16,32,1024]{2,1,0:T(8,128)(2,1)}), bf16[16,32,1024]{2,1,0:T(8,128)(2,1)S(1)}, u32[]{:S(2)}, u32[]{:S(2)}) async-start(bf16[16,32,1024]{2,1,0:T(8,128)(2,1)} %copy.29), calls=%async_computation.1 | async-start | bytes 2097152 | tf_op jit(solution)/shard_map/all_to_all | solution.py:90
  21.8 36.7 %all-to-all-done = bf16[16,32,1024]{2,1,0:T(8,128)(2,1)S(1)} async-done(((bf16[16,32,1024]{2,1,0:T(8,128)(2,1)}), bf16[16,32,1024]{2,1,0:T(8,128)(2,1)S(1)}, u32[]{:S(2)}, u32[]{:S(2)}) %all-to-all-start) | async-done | bytes 1048608 | tf_op jit(solution)/shard_map/all_to_all | solution.py:90
  60.9 12.2 %all-gather.7.cloned.1.call-done = bf16[1,1024,1024]{2,1,0:T(8,128)(2,1)} async-done(((bf16[1,128,1024]{2,1,0:T(8,128)(2,1)}), bf16[1,1024,1024]{2,1,0:T(8,128)(2,1)}) %all-gather.7.cloned.1.call-update) | async-done | bytes 2097168 | tf_op jit(solution)/shard_map/all_gather | solution.py:103
  73.1 63.3 %all-gather.5.cloned.1.call-done = bf16[1,1024,3,512]{1,3,2,0:T(8,128)(2,1)} async-done(((bf16[1,128,3,512]{1,3,2,0:T(8,128)(2,1)}), bf16[1,1024,3,512]{1,3,2,0:T(8,128)(2,1)}) %all-gather.5.cloned.1.call-update) | async-done | bytes 3145744 | tf_op jit(solution)/shard_map/all_gather | solution.py:102
  136.4 73.2 %all-gather.9.cloned.1.call-done = bf16[1,1024,2048]{2,1,0:T(8,128)(2,1)} async-done(((bf16[1,128,2048]{2,1,0:T(8,128)(2,1)}), bf16[1,1024,2048]{2,1,0:T(8,128)(2,1)}) %all-gather.9.cloned.1.call-update) | async-done | bytes 4194320 | tf_op jit(solution)/shard_map/all_gather | solution.py:104
  209.5 75.1 %all-gather.11.cloned.1.call-done = bf16[1,2048,1024]{2,1,0:T(8,128)(2,1)} async-done(((bf16[1,2048,128]{2,1,0:T(8,128)(2,1)}), bf16[1,2048,1024]{2,1,0:T(8,128)(2,1)}) %all-gather.11.cloned.1.call-update) | async-done | bytes 4194320 | tf_op jit(solution)/shard_map/all_gather | solution.py:105
  285.7 260.2 %while.18 = (s32[]{:T(128)}, bf16[4,32,512]{2,1,0:T(8,128)(2,1)S(1)}, bf16[4,4,32,1024]{3,2,1,0:T(8,128)(2,1)}, s32[]{:T(128)}, pred[]{:T(512)}, /*index=5*/bf16...) while((s32[]{:T(128)}, ...), condition=%wide.region_18.19_spmd.clone, body=%wide.region_4.18_spmd.clone.sunk | while | flops 1817675392 | bytes 26838016 | solution.py:181
  304.6 11.4 %conditional.7 = (f32[128,1024]{1,0:T(8,128)}, f32[128,1024]{1,0:T(8,128)S(1)}) conditional(s32[]{:T(128)} %convert_element_type.220, () %tuple.72, (bf16[4,32,1024]{2,1,0:T(8,128)(2,1)S(1)}, bf16[4,32,1024]{2,1,0:T(8,128)(2,1)S(1)}, bf16[1024,1024]{1,0:T(8,128)(2,1)}, bf16[1024]{0:T(1024)(128)(2,1)S(1)}, bf16[1024,2048]{1,0:T(8,128)(2,1)}, ...), branch_computations={%region_11.11_spmd, %region_12.14_spmd} | conditional | flops 1360790656 | bytes 13130256 | solution.py:166
  308.7 7.3 %fusion.29 = f32[128,1024]{1,0:T(8,128)S(1)} fusion(bf16[2048,1024]{1,0:T(8,128)(2,1)} %get-tuple-element.436, bf16[1024,2048]{1,0:T(8,128)(2,1)} %get-tuple-element.434, f32[2048]{0:T(1024)S(1)} %get-tuple-element.435, f32[128,1024]{1,0:T(8,128)} %get-tuple-element.704, f32[1024]{0:T(1024)S(1)} %convert_element_type.116, f32[128]{0:T(128)S(1)} %add_rsqrt_fusion.1, ...), kind=kOutput, calls=%fused_computation.50 | convolution fusion | flops 1091567616 | bytes 9450496 | tf_op jit(solution)/shard_map/while/body/eval_jaxpr/cond/branch_1_fun/dot_general | solution.py:160
  317.3 9.9 %reduce-scatter.2.cloned.1.call-done = bf16[128,512]{1,0:T(8,128)(2,1)} async-done(((bf16[128,1024]{1,0:T(8,128)(2,1)}), bf16[128,512]{1,0:T(8,128)(2,1)}) %reduce-scatter.2.cloned.1.call-update) | async-done | bytes 131088 | tf_op jit(solution)/shard_map/while/body/eval_jaxpr/reduce_scatter | solution.py:167
  330.3 6.5 %all_gather.40 = bf16[4,32,1024]{2,1,0:T(8,128)(2,1)S(1)} all-gather(bf16[4,32,512]{2,1,0:T(8,128)(2,1)S(1)} %get-tuple-element.728), channel_id=1, replica_groups=mesh['dp'=8,'section'=2,'tensor'=2] {'tensor'}, dimensions={2}, use_global_device_ids=true | all-gather | bytes 393216 | tf_op jit(solution)/shard_map/while/body/eval_jaxpr/all_gather | solution.py:119
  350.0 11.4 %conditional.7 = (f32[128,1024]{1,0:T(8,128)}, f32[128,1024]{1,0:T(8,128)S(1)}) conditional(s32[]{:T(128)} %convert_element_type.220, () %tuple.72, (bf16[4,32,1024]{2,1,0:T(8,128)(2,1)S(1)}, bf16[4,32,1024]{2,1,0:T(8,128)(2,1)S(1)}, bf16[1024,1024]{1,0:T(8,128)(2,1)}, bf16[1024]{0:T(1024)(128)(2,1)S(1)}, bf16[1024,2048]{1,0:T(8,128)(2,1)}, ...), branch_computations={%region_11.11_spmd, %region_12.14_spmd} | conditional | flops 1360790656 | bytes 13130256 | solution.py:166
  354.1 7.3 %fusion.29 = f32[128,1024]{1,0:T(8,128)S(1)} fusion(bf16[2048,1024]{1,0:T(8,128)(2,1)} %get-tuple-element.436, bf16[1024,2048]{1,0:T(8,128)(2,1)} %get-tuple-element.434, f32[2048]{0:T(1024)S(1)} %get-tuple-element.435, f32[128,1024]{1,0:T(8,128)} %get-tuple-element.704, f32[1024]{0:T(1024)S(1)} %convert_element_type.116, f32[128]{0:T(128)S(1)} %add_rsqrt_fusion.1, ...), kind=kOutput, calls=%fused_computation.50 | convolution fusion | flops 1091567616 | bytes 9450496 | tf_op jit(solution)/shard_map/while/body/eval_jaxpr/cond/branch_1_fun/dot_general | solution.py:160
  362.6 11.5 %reduce-scatter.2.cloned.1.call-done = bf16[128,512]{1,0:T(8,128)(2,1)} async-done(((bf16[128,1024]{1,0:T(8,128)(2,1)}), bf16[128,512]{1,0:T(8,128)(2,1)}) %reduce-scatter.2.cloned.1.call-update) | async-done | bytes 131088 | tf_op jit(solution)/shard_map/while/body/eval_jaxpr/reduce_scatter | solution.py:167
  377.2 6.5 %all_gather.40 = bf16[4,32,1024]{2,1,0:T(8,128)(2,1)S(1)} all-gather(bf16[4,32,512]{2,1,0:T(8,128)(2,1)S(1)} %get-tuple-element.728), channel_id=1, replica_groups=mesh['dp'=8,'section'=2,'tensor'=2] {'tensor'}, dimensions={2}, use_global_device_ids=true | all-gather | bytes 393216 | tf_op jit(solution)/shard_map/while/body/eval_jaxpr/all_gather | solution.py:119
  396.9 11.4 %conditional.7 = (f32[128,1024]{1,0:T(8,128)}, f32[128,1024]{1,0:T(8,128)S(1)}) conditional(s32[]{:T(128)} %convert_element_type.220, () %tuple.72, (bf16[4,32,1024]{2,1,0:T(8,128)(2,1)S(1)}, bf16[4,32,1024]{2,1,0:T(8,128)(2,1)S(1)}, bf16[1024,1024]{1,0:T(8,128)(2,1)}, bf16[1024]{0:T(1024)(128)(2,1)S(1)}, bf16[1024,2048]{1,0:T(8,128)(2,1)}, ...), branch_computations={%region_11.11_spmd, %region_12.14_spmd} | conditional | flops 1360790656 | bytes 13130256 | solution.py:166
  401.0 7.3 %fusion.29 = f32[128,1024]{1,0:T(8,128)S(1)} fusion(bf16[2048,1024]{1,0:T(8,128)(2,1)} %get-tuple-element.436, bf16[1024,2048]{1,0:T(8,128)(2,1)} %get-tuple-element.434, f32[2048]{0:T(1024)S(1)} %get-tuple-element.435, f32[128,1024]{1,0:T(8,128)} %get-tuple-element.704, f32[1024]{0:T(1024)S(1)} %convert_element_type.116, f32[128]{0:T(128)S(1)} %add_rsqrt_fusion.1, ...), kind=kOutput, calls=%fused_computation.50 | convolution fusion | flops 1091567616 | bytes 9450496 | tf_op jit(solution)/shard_map/while/body/eval_jaxpr/cond/branch_1_fun/dot_general | solution.py:160
  409.6 11.5 %reduce-scatter.2.cloned.1.call-done = bf16[128,512]{1,0:T(8,128)(2,1)} async-done(((bf16[128,1024]{1,0:T(8,128)(2,1)}), bf16[128,512]{1,0:T(8,128)(2,1)}) %reduce-scatter.2.cloned.1.call-update) | async-done | bytes 131088 | tf_op jit(solution)/shard_map/while/body/eval_jaxpr/reduce_scatter | solution.py:167
  443.9 11.4 %conditional.7 = (f32[128,1024]{1,0:T(8,128)}, f32[128,1024]{1,0:T(8,128)S(1)}) conditional(s32[]{:T(128)} %convert_element_type.220, () %tuple.72, (bf16[4,32,1024]{2,1,0:T(8,128)(2,1)S(1)}, bf16[4,32,1024]{2,1,0:T(8,128)(2,1)S(1)}, bf16[1024,1024]{1,0:T(8,128)(2,1)}, bf16[1024]{0:T(1024)(128)(2,1)S(1)}, bf16[1024,2048]{1,0:T(8,128)(2,1)}, ...), branch_computations={%region_11.11_spmd, %region_12.14_spmd} | conditional | flops 1360790656 | bytes 13130256 | solution.py:166
  448.0 7.3 %fusion.29 = f32[128,1024]{1,0:T(8,128)S(1)} fusion(bf16[2048,1024]{1,0:T(8,128)(2,1)} %get-tuple-element.436, bf16[1024,2048]{1,0:T(8,128)(2,1)} %get-tuple-element.434, f32[2048]{0:T(1024)S(1)} %get-tuple-element.435, f32[128,1024]{1,0:T(8,128)} %get-tuple-element.704, f32[1024]{0:T(1024)S(1)} %convert_element_type.116, f32[128]{0:T(128)S(1)} %add_rsqrt_fusion.1, ...), kind=kOutput, calls=%fused_computation.50 | convolution fusion | flops 1091567616 | bytes 9450496 | tf_op jit(solution)/shard_map/while/body/eval_jaxpr/cond/branch_1_fun/dot_general | solution.py:160
  456.5 11.5 %reduce-scatter.2.cloned.1.call-done = bf16[128,512]{1,0:T(8,128)(2,1)} async-done(((bf16[128,1024]{1,0:T(8,128)(2,1)}), bf16[128,512]{1,0:T(8,128)(2,1)}) %reduce-scatter.2.cloned.1.call-update) | async-done | bytes 131088 | tf_op jit(solution)/shard_map/while/body/eval_jaxpr/reduce_scatter | solution.py:167
  486.4 26.6 %reduce-scatter.2.cloned.1.call-done = bf16[128,512]{1,0:T(8,128)(2,1)} async-done(((bf16[128,1024]{1,0:T(8,128)(2,1)}), bf16[128,512]{1,0:T(8,128)(2,1)}) %reduce-scatter.2.cloned.1.call-update) | async-done | bytes 131088 | tf_op jit(solution)/shard_map/while/body/eval_jaxpr/reduce_scatter | solution.py:167
  531.5 11.4 %reduce-scatter.2.cloned.1.call-done = bf16[128,512]{1,0:T(8,128)(2,1)} async-done(((bf16[128,1024]{1,0:T(8,128)(2,1)}), bf16[128,512]{1,0:T(8,128)(2,1)}) %reduce-scatter.2.cloned.1.call-update) | async-done | bytes 131088 | tf_op jit(solution)/shard_map/while/body/eval_jaxpr/reduce_scatter | solution.py:167
  547.9 20.0 %all-reduce.2.cloned.1.call-done = bf16[16,32,512]{2,1,0:T(8,128)(2,1)} async-done(((bf16[16,32,512]{2,1,0:T(8,128)(2,1)}), bf16[16,32,512]{2,1,0:T(8,128)(2,1)}) %all-reduce.2.cloned.1.call-update) | async-done | bytes 524304 | tf_op jit(solution)/shard_map/psum | solution.py:20
  (230 shorter events, 177.6 us)
Async XLA Ops:
  6.5 66.6 %all-gather.7.cloned.1.call-start = ((), (), s32[]{:S(2)}) async-start(), calls=%async_computation.3 | async-start | bytes 2359296 | tf_op jit(solution)/shard_map/all_gather | solution.py:103
  7.3 129.1 %all-gather.5.cloned.1.call-start = ((), (), s32[]{:S(2)}) async-start(), calls=%async_computation.2 | async-start | bytes 3538944 | tf_op jit(solution)/shard_map/all_gather | solution.py:102
  9.3 200.3 %all-gather.9.cloned.1.call-start = ((), (), s32[]{:S(2)}) async-start(), calls=%async_computation.4 | async-start | bytes 4718592 | tf_op jit(solution)/shard_map/all_gather | solution.py:104
  10.0 274.6 %all-gather.11.cloned.1.call-start = ((), (), s32[]{:S(2)}) async-start(), calls=%async_computation.5 | async-start | bytes 4718592 | tf_op jit(solution)/shard_map/all_gather | solution.py:105
  11.6 9.7 %copy-start.6 = (s32[128]{0:T(128)S(1)}, s32[128]{0:T(128)}, u32[]{:S(2)}) copy-start(s32[128]{0:T(128)} %param.19) | copy-start | bytes 1540
  11.7 9.8 %copy-start.5 = (s32[128]{0:T(128)S(1)}, s32[128]{0:T(128)}, u32[]{:S(2)}) copy-start(s32[128]{0:T(128)} %param.18) | copy-start | bytes 1540
  11.7 10.1 %copy-start.2 = (bf16[1,2048]{1,0:T(2,128)(2,1)S(1)}, bf16[1,2048]{1,0:T(2,128)(2,1)}, u32[]{:S(2)}) copy-start(bf16[1,2048]{1,0:T(2,128)(2,1)} %param.23) | copy-start | bytes 12292
  11.7 10.1 %copy-start.3 = (bf16[1,1024]{1,0:T(2,128)(2,1)S(1)}, bf16[1,1024]{1,0:T(2,128)(2,1)}, u32[]{:S(2)}) copy-start(bf16[1,1024]{1,0:T(2,128)(2,1)} %param.25) | copy-start | bytes 6148
  11.7 10.1 %copy-start.4 = (bf16[1,1024]{1,0:T(2,128)(2,1)S(1)}, bf16[1,1024]{1,0:T(2,128)(2,1)}, u32[]{:S(2)}) copy-start(bf16[1,1024]{1,0:T(2,128)(2,1)} %param.26) | copy-start | bytes 6148
  14.1 44.5 %all-to-all-start = ((bf16[16,32,1024]{2,1,0:T(8,128)(2,1)}), bf16[16,32,1024]{2,1,0:T(8,128)(2,1)S(1)}, u32[]{:S(2)}, u32[]{:S(2)}) async-start(bf16[16,32,1024]{2,1,0:T(8,128)(2,1)} %copy.29), calls=%async_computation.1 | async-start | bytes 2097152 | tf_op jit(solution)/shard_map/all_to_all | solution.py:90
  21.4 264.4 %copy-start.1 = (bf16[1024]{0:T(1024)(128)(2,1)S(1)}, bf16[1024]{0:T(1024)(128)(2,1)}, u32[]{:S(2)}) copy-start(bf16[1024]{0:T(1024)(128)(2,1)} %param.27) | copy-start | bytes 6148
  285.8 41.4 %reduce-scatter.2.cloned.1.call-start = ((), (), s32[]{:S(2)}) async-start(), calls=%async_computation.7 | async-start | bytes 393216 | tf_op jit(solution)/shard_map/while/body/eval_jaxpr/reduce_scatter | solution.py:167
  328.2 2.0 collective-permute-start
  330.3 43.9 %reduce-scatter.2.cloned.1.call-start = ((), (), s32[]{:S(2)}) async-start(), calls=%async_computation.7 | async-start | bytes 393216 | tf_op jit(solution)/shard_map/while/body/eval_jaxpr/reduce_scatter | solution.py:167
  375.2 2.0 collective-permute-start
  377.2 43.9 %reduce-scatter.2.cloned.1.call-start = ((), (), s32[]{:S(2)}) async-start(), calls=%async_computation.7 | async-start | bytes 393216 | tf_op jit(solution)/shard_map/while/body/eval_jaxpr/reduce_scatter | solution.py:167
  422.1 2.0 collective-permute-start
  424.1 43.9 %reduce-scatter.2.cloned.1.call-start = ((), (), s32[]{:S(2)}) async-start(), calls=%async_computation.7 | async-start | bytes 393216 | tf_op jit(solution)/shard_map/while/body/eval_jaxpr/reduce_scatter | solution.py:167
  469.0 2.0 collective-permute-start
  471.1 41.9 %reduce-scatter.2.cloned.1.call-start = ((), (), s32[]{:S(2)}) async-start(), calls=%async_computation.7 | async-start | bytes 393216 | tf_op jit(solution)/shard_map/while/body/eval_jaxpr/reduce_scatter | solution.py:167
  514.1 2.0 collective-permute-start
  516.1 26.8 %reduce-scatter.2.cloned.1.call-start = ((), (), s32[]{:S(2)}) async-start(), calls=%async_computation.7 | async-start | bytes 393216 | tf_op jit(solution)/shard_map/while/body/eval_jaxpr/reduce_scatter | solution.py:167
  544.0 2.0 collective-permute-start
  546.0 21.9 %all-reduce.2.cloned.1.call-start = ((), (), s32[]{:S(2)}) async-start(), calls=%async_computation.6 | async-start | bytes 1048576 | tf_op jit(solution)/shard_map/psum | solution.py:20
  (1 other events, 5.1 us)
Sparse Core Ops, SparseCore 0:
  9.5 63.6 all-gather.6
  75.2 61.1 all-gather.4
  138.5 70.9 all-gather.8
  211.4 73.1 all-gather.10
  316.9 10.2 reduce-scatter.1
  362.3 11.7 reduce-scatter.1
  409.2 11.7 reduce-scatter.1
  456.2 11.7 reduce-scatter.1
  486.1 26.8 reduce-scatter.1
  531.1 11.7 reduce-scatter.1
  549.1 18.7 all-reduce.1
where the time goes:
time: 577 us; the launch traced here: 576 us
  waiting for transfers between devices  365 us (63%)
  blocking collectives  72.4 us (13%)
  matrix products  64.4 us (11%)
  other arithmetic  41.1 us (7%)
  between operations  13.2 us (2%)
  local copies, waits for them, and re-layouts  11.3 us (2%)
  starting transfers between devices  7.91 us (1%)
    reduce_scatter x6, waiting for transfers between devices, advance(): lax.psum_scatter(partial_value.astype(jnp.bfloat16), 'tensor', scatter_di...  82.3 us
    all_gather x1, waiting for transfers between devices, local(): lax.all_gather(down_weight, 'dp', axis=2, tiled=True)  75.1 us
    all_gather x1, waiting for transfers between devices, local(): lax.all_gather(up_weight, 'dp', axis=1, tiled=True)  73.2 us
    all_gather x1, waiting for transfers between devices, local(): lax.all_gather(qkv_weight, 'dp', axis=1, tiled=True)  63.3 us
    all_gather x6, blocking collectives, advance(): current = lax.all_gather(carried, 'tensor', axis=2, tiled=True)  38.3 us
    all_to_all x1, waiting for transfers between devices, local(): lax.all_to_all(outgoing, 'dp', split_axis=0, concat_axis=0, tiled=True)  36.7 us
    all_gather x6, blocking collectives, advance(): joined = lax.all_gather(head_out, 'tensor', axis=2, tiled=True)  34 us
    dot_general x4, matrix products, mlp_part(): jnp.dot(hidden, down_full, preferred_element_type=jnp.float32)  29.2 us
  transfers between devices with their start and end apart: 18, of which 12 were waited for; matrix products, arithmetic and copies ran while one was open for 4% of the time, Pallas kernels for 0%

commit v1 on v0

v1 whole, which is shorter than its diff:
```python
import functools

import jax
import jax.numpy as jnp
from jax import lax
from jax.experimental import pallas as pl
from jax.experimental.pallas import tpu as pltpu
from jax.sharding import PartitionSpec as P

HEAD_DIM = 64
CHUNK = 128
TILE = 256
epsilon = 1e-06
BF = jnp.bfloat16
F32 = jnp.float32


def normalised(values, gain_row):
    average = jnp.mean(values, axis=-1, keepdims=True)
    centred = values - average
    spread = jnp.mean(centred * centred, axis=-1, keepdims=True)
    return centred * lax.rsqrt(spread + epsilon) * gain_row


def encoder(
    groups,
    cap_rows,
    tok,
    select,
    pick,
    mask,
    bias,
    gain_attn,
    gain_mlp,
    gain_final,
    w_qkv,
    w_out,
    w_up,
    w_down,
    o_ref,
    g_qkv,
    g_out,
    g_up,
    g_down,
    outgoing,
    received,
    x,
    normed,
    merged,
    ho_mine,
    ho_other,
    mid,
    hidden,
    p_mine,
    p_other,
    stream,
    fin,
    tok_ss,
    tok_rs,
    own_s,
    line_up,
    line_down,
    line_rs,
    pair_ss,
    pair_rs,
    ho_ss,
    ho_rs,
    p_ss,
    p_rs,
    x_ss,
    x_rs,
    fin_s,
    go_sem,
):
    me = lax.axis_index("dp")
    section = lax.axis_index("section")
    tensor = lax.axis_index("tensor")
    half = groups // 2
    high, low = me // 2, me % 2
    rows, width = tok.shape
    quarter = ho_mine.shape[1]
    images, section_rows, _ = o_ref.shape
    block = fin.shape[1]
    above = {"dp": jnp.minimum(high + 1, half - 1) * 2 + low}
    below = {"dp": jnp.maximum(high - 1, 0) * 2 + low}
    pair = {"dp": high * 2 + 1 - low}
    beside = {"tensor": 1 - tensor}
    partner = {"section": 1 - section}

    def remote(src, dst, ss, rs, device):
        return pltpu.make_async_remote_copy(
            src_ref=src,
            dst_ref=dst,
            send_sem=ss,
            recv_sem=rs,
            device_id=device,
            device_id_type=pl.DeviceIdType.MESH,
        )

    barrier = pltpu.get_barrier_semaphore()
    for step in range(1, groups):
        pl.semaphore_signal(
            barrier,
            inc=1,
            device_id={"dp": (me + step) % groups},
            device_id_type=pl.DeviceIdType.MESH,
        )
    for device in (beside, partner):
        pl.semaphore_signal(
            barrier, inc=1, device_id=device, device_id_type=pl.DeviceIdType.MESH
        )
    pl.semaphore_wait(barrier, groups + 1)

    weights = ((w_qkv, g_qkv), (w_out, g_out), (w_up, g_up), (w_down, g_down))
    narrow = len(g_down.shape) == 3

    def piece(which, number):
        source, whole = weights[which]
        if which < 3:
            size = source.shape[0]
            return whole.at[pl.ds(pl.multiple_of(number * size, size), size), :]
        size = source.shape[1]
        if narrow:
            return whole.at[number]
        return whole.at[:, pl.ds(pl.multiple_of(number * size, size), size)]

    def slot(buffer, number):
        return buffer.at[pl.ds(pl.multiple_of(number * cap_rows, cap_rows), cap_rows), :]

    first = section == 0
    second = section == 1

    def token_copy(step):
        peer = (me + step) % groups
        return remote(
            slot(outgoing, peer), slot(received, me), tok_ss.at[peer], tok_rs.at[me], {"dp": peer}
        )

    def token_arrival(step):
        peer = (me + step) % groups
        return remote(
            slot(outgoing, peer), slot(received, peer), tok_ss.at[peer], tok_rs.at[peer], {"dp": peer}
        )

    own_tokens = pltpu.make_async_copy(slot(outgoing, me), slot(received, me), tok_ss.at[me])

    @pl.when(first)
    def _():
        slots = outgoing.shape[0]

        @pl.loop(0, width // TILE)
        def _(tile):
            columns = pl.ds(pl.multiple_of(tile * TILE, TILE), TILE)
            outgoing[:, columns] = jnp.dot(
                select[...], tok[:, columns], preferred_element_type=F32
            ).astype(BF)

        for step in range(1, groups):
            token_copy(step).start()
        own_tokens.start()

    @pl.when(second)
    def _():
        pl.semaphore_wait(go_sem, 1)

    owns = []
    for which in range(4):
        own = pltpu.make_async_copy(weights[which][0], piece(which, me), own_s.at[which])
        own.start()
        owns.append(own)

    def up_copy(which, source_high, src):
        return remote(
            src,
            piece(which, source_high * 2 + low),
            line_up.at[which, source_high],
            line_rs.at[which, source_high],
            above,
        )

    def down_copy(which, source_high, src):
        return remote(
            src,
            piece(which, source_high * 2 + low),
            line_down.at[which, source_high],
            line_rs.at[which, source_high],
            below,
        )

    def pair_copy(which, source_high, src):
        return remote(
            src,
            piece(which, source_high * 2 + low),
            pair_ss.at[which, source_high],
            pair_rs.at[which, source_high],
            pair,
        )

    has_above = high < half - 1
    has_below = high > 0
    for which in range(4):
        source = weights[which][0]

        @pl.when(has_above)
        def _():
            up_copy(which, high, source).start()

        @pl.when(has_below)
        def _():
            down_copy(which, high, source).start()

        pair_copy(which, high, source).start()

    def relay(which, back):
        lower = high - back

        @pl.when(lower >= 0)
        def _():
            src = piece(which, lower * 2 + low)
            arriving = up_copy(which, lower, src)
            arriving.wait_recv()

            @pl.when(has_above)
            def _():
                up_copy(which, lower, src).start()

            pair_copy(which, lower, src).start()

        upper = high + back

        @pl.when(upper < half)
        def _():
            src = piece(which, upper * 2 + low)
            arriving = down_copy(which, upper, src)
            arriving.wait_recv()

            @pl.when(has_below)
            def _():
                down_copy(which, upper, src).start()

            pair_copy(which, upper, src).start()

    for back in range(1, half):
        for which in range(4):
            relay(which, back)

    @pl.when(first)
    def _():
        pl.semaphore_signal(
            go_sem, inc=1, device_id=partner, device_id_type=pl.DeviceIdType.MESH
        )

    def gathered(which):
        owns[which].wait()
        for source_high in range(half):
            other = piece(which, source_high * 2 + 1 - low)
            remote(
                other, other, pair_ss.at[which, source_high], pair_rs.at[which, source_high], pair
            ).wait_recv()

    chunks = rows // CHUNK

    def chunk_rows(chunk):
        return pl.ds(pl.multiple_of(chunk * CHUNK, CHUNK), CHUNK)

    def stream_copy(part):
        at = pl.ds(part * TILE, TILE)
        return remote(
            stream.at[at, :], x.at[at, :], x_ss.at[part], x_rs.at[part], partner
        )

    parts = rows // TILE

    @pl.when(first)
    def _():
        for step in range(1, groups):
            token_arrival(step).wait_recv()
        own_tokens.wait()

        @pl.loop(0, width // TILE)
        def _(tile):
            columns = pl.ds(pl.multiple_of(tile * TILE, TILE), TILE)
            x[:, columns] = jnp.dot(
                pick[...], received[:, columns], preferred_element_type=F32
            ).astype(BF)

    for which in range(4):
        gathered(which)

    @pl.when(second)
    def _():
        for part in range(parts):
            stream_copy(part).wait_recv()

    @pl.loop(0, chunks)
    def _(chunk):
        at = chunk_rows(chunk)
        normed[at, :] = normalised(x[at, :].astype(F32), gain_attn[...]).astype(BF)

    @pl.loop(0, merged.shape[1] // TILE)
    def _(tile):
        columns = pl.ds(pl.multiple_of(tile * TILE, TILE), TILE)
        merged[:, columns] = jnp.dot(normed[...], g_qkv[:, columns], preferred_element_type=F32)

    lanes = 2 * HEAD_DIM
    lane_of = lax.broadcasted_iota(jnp.int32, (CHUNK, lanes), 1)
    contract = (((1,), (1,)), ((), ()))

    def head_copy(chunk):
        at = chunk_rows(chunk)
        return remote(
            ho_mine.at[at, :], ho_other.at[at, :], ho_ss.at[chunk], ho_rs.at[chunk], beside
        )

    @pl.loop(0, chunks)
    def _(chunk):
        at = chunk_rows(chunk)
        hidden_keys = mask[chunk]
        for two in range(quarter // lanes):
            q = merged[at, two * lanes : (two + 1) * lanes]
            k = merged[at, quarter + two * lanes : quarter + (two + 1) * lanes]
            v = merged[at, 2 * quarter + two * lanes : 2 * quarter + (two + 1) * lanes].astype(BF)
            k_top = k.astype(BF)
            k_rest = (k - k_top.astype(F32)).astype(BF)
            outs = []
            for head in range(2):
                mine = (lane_of < HEAD_DIM) if head == 0 else (lane_of >= HEAD_DIM)
                q_head = jnp.where(mine, q, 0.0)
                q_top = q_head.astype(BF)
                q_rest = (q_head - q_top.astype(F32)).astype(BF)
                scores = (
                    lax.dot_general(q_top, k_top, contract, preferred_element_type=F32)
                    + lax.dot_general(q_top, k_rest, contract, preferred_element_type=F32)
                    + lax.dot_general(q_rest, k_top, contract, preferred_element_type=F32)
                ) * HEAD_DIM ** (-0.5)
                scores = scores + hidden_keys
                scores = scores - jnp.max(scores, axis=-1, keepdims=True)
                powers = jnp.exp(scores)
                total = jnp.sum(powers, axis=-1, keepdims=True)
                mixed = jnp.dot(powers.astype(BF), v, preferred_element_type=F32)
                outs.append(mixed / total)
            ho_mine[at, two * lanes : (two + 1) * lanes] = jnp.where(
                lane_of < HEAD_DIM, outs[0], outs[1]
            ).astype(BF)
        head_copy(chunk).start()

    @pl.loop(0, chunks)
    def _(chunk):
        head_copy(chunk).wait()

    mine_rows = pl.ds(pl.multiple_of(tensor * quarter, quarter), quarter)
    other_rows = pl.ds(pl.multiple_of((1 - tensor) * quarter, quarter), quarter)

    @pl.loop(0, width // TILE)
    def _(tile):
        columns = pl.ds(pl.multiple_of(tile * TILE, TILE), TILE)
        mid[:, columns] = (
            x[:, columns].astype(F32)
            + jnp.dot(ho_mine[...], g_out[mine_rows, columns], preferred_element_type=F32)
            + jnp.dot(ho_other[...], g_out[other_rows, columns], preferred_element_type=F32)
        )

    @pl.loop(0, chunks)
    def _(chunk):
        at = chunk_rows(chunk)
        normed[at, :] = normalised(mid[at, :], gain_mlp[...]).astype(BF)

    @pl.loop(0, hidden.shape[1] // TILE)
    def _(tile):
        columns = pl.ds(pl.multiple_of(tile * TILE, TILE), TILE)
        raised = (
            jnp.dot(normed[...], g_up[:, columns], preferred_element_type=F32) + bias[:, columns]
        )
        hidden[:, columns] = (raised * (1.0 + lax.erf(raised * (0.5**0.5))) * 0.5).astype(BF)

    def partial_copy(part):
        at = pl.ds(part * TILE, TILE)
        return remote(p_mine.at[at, :], p_other.at[at, :], p_ss.at[part], p_rs.at[part], beside)

    for part in range(parts):
        at = pl.ds(part * TILE, TILE)

        @pl.loop(0, width // TILE)
        def _(tile):
            columns = pl.ds(pl.multiple_of(tile * TILE, TILE), TILE)
            if narrow:
                count = TILE // g_down.shape[2]
                product = jnp.concatenate(
                    [
                        jnp.dot(
                            hidden[at, :], g_down[tile * count + i], preferred_element_type=F32
                        )
                        for i in range(count)
                    ],
                    axis=1,
                )
            else:
                product = jnp.dot(hidden[at, :], g_down[:, columns], preferred_element_type=F32)
            p_mine[at, columns] = product.astype(BF)

        partial_copy(part).start()

    for part in range(parts):
        at = pl.ds(part * TILE, TILE)
        partial_copy(part).wait()
        stream[at, :] = (
            mid[at, :] + (p_mine[at, :].astype(F32) + p_other[at, :].astype(F32))
        ).astype(BF)

        @pl.when(first)
        def _():
            stream_copy(part).start()

    result = remote(
        fin.at[:, pl.ds(0, section_rows), :], o_ref, fin_s.at[0], fin_s.at[1], partner
    )

    @pl.when(second)
    def _():
        per = CHUNK // block
        own_columns = pl.ds(pl.multiple_of(tensor * quarter, quarter), quarter)

        @pl.loop(0, chunks)
        def _(chunk):
            at = chunk_rows(chunk)
            values = stream[at, :].astype(F32)
            average = jnp.mean(values, axis=-1, keepdims=True)
            centred = values - average
            scale = lax.rsqrt(jnp.mean(centred * centred, axis=-1, keepdims=True) + epsilon)
            piece_values = (
                (stream[at, own_columns].astype(F32) - average) * scale * gain_final[:, own_columns]
            )
            fin[pl.ds(chunk * per, per)] = piece_values.astype(BF).reshape(per, block, quarter)

        result.start()
        o_ref[...] = fin[:, section_rows:, :]
        result.wait_send()

    @pl.when(first)
    def _():
        for part in range(parts):
            stream_copy(part).wait_send()
        for step in range(1, groups):
            token_copy(step).wait_send()
        result.wait_recv()

    for which in range(4):
        source = weights[which][0]
        for back in range(half):

            @pl.when(has_above & (high - back >= 0))
            def _():
                up_copy(which, high - back, source).wait_send()

            @pl.when(has_below & (high + back < half))
            def _():
                down_copy(which, high + back, source).wait_send()

            pair_copy(which, back, source).wait_send()


def local(
    tokens,
    counts,
    assign,
    qkv_weight,
    out_weight,
    up_weight,
    up_bias,
    down_weight,
    attn_gain,
    mlp_gain,
    final_gain,
):
    groups = lax.axis_size("dp")
    sections = lax.axis_size("section")
    tensor_ranks = lax.axis_size("tensor")
    images_dev, block, width = tokens.shape
    quarter = width // tensor_ranks
    capacity = (images_dev + groups - 1) // groups
    total_images = assign.shape[0]
    rows = images_dev * block
    slots = groups * capacity
    my_group = lax.axis_index("dp")
    numbers = jnp.arange(total_images, dtype=jnp.int32)
    matches = (assign[:, None] == numbers[None, :]).astype(jnp.int32)
    slot_of = jnp.sum(matches * numbers[:, None], axis=0)
    target = slot_of // images_dev
    source_group = numbers // images_dev
    earlier = (
        (source_group[:, None] == source_group[None, :])
        & (target[:, None] == target[None, :])
        & (numbers[None, :] < numbers[:, None])
    )
    rank_all = jnp.sum(earlier.astype(jnp.int32), axis=1)
    send_slot = lax.dynamic_slice_in_dim(
        target * capacity + rank_all, my_group * images_dev, images_dev
    )
    my_images = lax.dynamic_slice_in_dim(assign, my_group * images_dev, images_dev)
    chosen = (my_images[:, None] == numbers[None, :]).astype(jnp.int32)
    receive_slot = jnp.sum(chosen * (source_group * capacity + rank_all)[None, :], axis=1)
    live_counts = jnp.sum(chosen * counts[None, :], axis=1)
    within = jnp.tile(jnp.arange(block, dtype=jnp.int32), images_dev)
    buffer_rows = jnp.arange(slots * block, dtype=jnp.int32)
    send_rows = jnp.repeat(send_slot, block) * block + within
    receive_rows = jnp.repeat(receive_slot, block) * block + within
    select = (buffer_rows[:, None] == send_rows[None, :]).astype(BF)
    pick = (buffer_rows[None, :] == receive_rows[:, None]).astype(BF)
    per = CHUNK // block
    key_live = within.reshape(-1, CHUNK) < jnp.repeat(live_counts, block).reshape(-1, CHUNK)
    image_of = jnp.arange(CHUNK) // block
    visible = key_live[:, None, :] & (image_of[:, None] == image_of[None, :])[None]
    mask = jnp.where(visible, 0.0, -1e30).astype(F32)
    w_qkv = qkv_weight[0].reshape(qkv_weight.shape[1], -1)
    w_out, w_up, w_down = out_weight[0], up_weight[0], down_weight[0]
    units = w_up.shape[1]
    down_columns = w_down.shape[1]
    down_shape = (units, width) if down_columns % 128 == 0 else (groups, units, down_columns)
    half = groups // 2
    cap_rows = capacity * block
    vmem = pl.BlockSpec(memory_space=pltpu.VMEM)
    anywhere = pl.BlockSpec(memory_space=pl.ANY)
    dma = pltpu.SemaphoreType.DMA
    section_rows = block // sections
    encoded = pl.pallas_call(
        functools.partial(encoder, groups, cap_rows),
        out_shape=jax.ShapeDtypeStruct((images_dev, section_rows, quarter), BF),
        in_specs=[vmem] * 8 + [anywhere] * 4,
        out_specs=vmem,
        scratch_shapes=[
            pltpu.VMEM((width, w_qkv.shape[1]), BF),
            pltpu.VMEM((width, width), BF),
            pltpu.VMEM((width, units), BF),
            pltpu.VMEM(down_shape, BF),
            pltpu.VMEM((slots * block, width), BF),
            pltpu.VMEM((slots * block, width), BF),
            pltpu.VMEM((rows, width), BF),
            pltpu.VMEM((rows, width), BF),
            pltpu.VMEM((rows, w_qkv.shape[1]), F32),
            pltpu.VMEM((rows, quarter), BF),
            pltpu.VMEM((rows, quarter), BF),
            pltpu.VMEM((rows, width), F32),
            pltpu.VMEM((rows, units), BF),
            pltpu.VMEM((rows, width), BF),
            pltpu.VMEM((rows, width), BF),
            pltpu.VMEM((rows, width), BF),
            pltpu.VMEM((images_dev, block, quarter), BF),
            dma((groups,)),
            dma((groups,)),
            dma((4,)),
            dma((4, half)),
            dma((4, half)),
            dma((4, half)),
            dma((4, half)),
            dma((4, half)),
            dma((rows // CHUNK,)),
            dma((rows // CHUNK,)),
            dma((rows // TILE,)),
            dma((rows // TILE,)),
            dma((rows // TILE,)),
            dma((rows // TILE,)),
            dma((2,)),
            pltpu.SemaphoreType.REGULAR,
        ],
        compiler_params=pltpu.CompilerParams(
            collective_id=0, has_side_effects=True, vmem_limit_bytes=60 * 1024 * 1024
        ),
    )(
        tokens.reshape(rows, width),
        select,
        pick,
        mask,
        up_bias[0].astype(F32)[None],
        attn_gain[0].astype(F32)[None],
        mlp_gain[0].astype(F32)[None],
        final_gain.astype(F32)[None],
        w_qkv,
        w_out,
        w_up,
        w_down,
    )
    row_numbers = lax.axis_index("section") * section_rows + jnp.arange(section_rows)
    alive = row_numbers[None, :, None] < live_counts[:, None, None]
    return jnp.where(alive, encoded, jnp.zeros_like(encoded))


def solution(mesh):
    in_specs = (
        P("dp", None, None),
        P(),
        P(),
        P("section", "dp", None, "tensor"),
        P("section", "dp", None),
        P("section", "dp", "tensor"),
        P("section", "tensor"),
        P("section", "tensor", "dp"),
        P("section", None),
        P("section", None),
        P(),
    )
    out_specs = P("dp", "section", "tensor")
    return jax.shard_map(local, mesh=mesh, in_specs=in_specs, out_specs=out_specs, check_vma=False)
```

time: 577 us -> 225 us (0.39)
  waiting for transfers between devices: 365 us -> 0 us
  Pallas kernels: 0 us -> 210 us
  blocking collectives: 72.4 us -> 0 us
  matrix products: 64.4 us -> 0 us
  other arithmetic: 41.1 us -> 11.7 us
  between operations: 13.2 us -> 0.04 us
  local copies, waits for them, and re-layouts: 11.3 us -> 2.37 us
  starting transfers between devices: 7.91 us -> 0 us
    all_gather x4 -> x0, waiting for transfers between devices: 224 us -> none  [the longest x1 75.1 us: local(): lax.all_gather(down_weight, 'dp', axis=2, tiled=True)]
    pallas_call x0 -> x1, Pallas kernels: none -> 210 us  [local(): pl.pallas_call(functools.partial(encoder, groups, cap_rows), out_shape=ja...]
    reduce_scatter x6 -> x0, waiting for transfers between devices: 82.3 us -> none  [advance(): lax.psum_scatter(partial_value.astype(jnp.bfloat16), 'tensor', scatter_di...]
    all_gather x12 -> x0, blocking collectives: 72.4 us -> none  [the longest x6 38.3 us: advance(): current = lax.all_gather(carried, 'tensor', axis=2, tiled=True)]
    dot_general x22 -> x0, matrix products: 64.4 us -> none  [the longest x4 29.2 us: mlp_part(): jnp.dot(hidden, down_full, preferred_element_type=jnp.float32)]
    all_to_all x1 -> x0, waiting for transfers between devices: 36.7 us -> none  [local(): lax.all_to_all(outgoing, 'dp', split_axis=0, concat_axis=0, tiled=True)]
    psum x1 -> x0, waiting for transfers between devices: 20 us -> none  [broadcast(): return lax.psum(jnp.where(mine, value, jnp.zeros_like(value)), axis)]
    select_n x14 -> x4, other arithmetic: 19.5 us -> 2.5 us  [the longest x1 1.76 us: local(): return jnp.where(alive, encoded, jnp.zeros_like(encoded))]
  transfers between devices with their start and end apart: 18 -> 0, of which waited for: 12 -> 0; matrix products, arithmetic and copies ran while one was open for 4% -> 0% of each run, Pallas kernels for 0% -> 0%
where the time goes in v1:
time: 225 us; the launch traced here: 224 us
  Pallas kernels  210 us (93%)
  other arithmetic  11.7 us (5%)
  local copies, waits for them, and re-layouts  2.37 us (1%)
    pallas_call x1, Pallas kernels, local(): pl.pallas_call(functools.partial(encoder, groups, cap_rows), out_shape=ja...  210 us

profile of v1, /device:TPU:0, one launch (start us, length us, event | category | flops | bytes accessed | tf_op | source)
XLA Modules:
  0.0 224.5 jit_solution(17204765824435878196)
XLA Ops:
  0.0 0.8 select_reduce_fusion
  0.8 0.7 dynamic_slice.6
  1.6 0.2 convert_reduce_fusion
  1.7 0.1 dynamic-slice_multiply_fusion
  1.8 0.8 select_reduce_fusion.2
  2.7 0.1 broadcast_compare_fusion.1
  2.7 0.1 broadcast_in_dim.32
  2.8 0.1 tile.18
  2.9 1.3 convert_element_type.28.gain_attn
  4.2 1.3 convert_element_type.29.gain_mlp
  5.5 1.3 broadcast_in_dim.74
  6.8 0.1 broadcast_in_dim.34
  6.9 0.1 iota_add_fusion
  7.0 0.1 add.82
  7.1 0.1 add.79
  7.2 1.3 convert_element_type.27.bias
  8.5 0.1 broadcast_compare_fusion
  8.6 0.7 and_select_fusion.mask
  9.3 0.2 copy.15
  9.6 0.9 copy.16.w_qkv
  10.5 0.9 fusion.select
  11.4 1.0 fusion.1.pick
  12.4 210.3 %shard_map.109 = bf16[16,16,512]{2,1,0:T(8,128)(2,1)} custom-call(bf16[512,1024]{1,0:T(8,128)(2,1)} %bitcast.7, bf16[512,512]{1,0:T(8,128)(2,1)} %fusion.select, bf16[512,512]{1,0:T(8,128)(2,1)} %fusion.1.pick, f32[4,128,128]{2,1,0:T(8,128)} %and_select_fusion.mask, f32[1,2048]{1,0:T(1,128)} %convert_element_type.27.bias, ...), custom_call_target="tpu_custom_call" | custom-call | tf_op jit(solution)/shard_map/pallas_call | solution.py:525
  222.7 1.8 broadcast_select_fusion
  (11 shorter events, 0.2 us)
Async XLA Ops:
  0.0 9.3 %copy-start = (bf16[1,128,3,512]{3,1,2,0:T(8,128)(2,1)S(1)}, bf16[1,128,3,512]{3,1,2,0:T(8,128)(2,1)}, u32[]{:S(2)}) copy-start(bf16[1,128,3,512]{3,1,2,0:T(8,128)(2,1)} %param.14) | copy-start | bytes 1179652

commit v2 on v1

--- a/solution.py
+++ b/solution.py
@@ -70,6 +70,9 @@
     x_ss,
     x_rs,
     fin_s,
+    lend_ss,
+    lend_rs,
+    swap_s,
     go_sem,
 ):
     me = lax.axis_index("dp")
@@ -111,17 +114,21 @@
         )
     pl.semaphore_wait(barrier, groups + 1)
 
-    weights = ((w_qkv, g_qkv), (w_out, g_out), (w_up, g_up), (w_down, g_down))
     narrow = len(g_down.shape) == 3
+    mine_columns = pl.ds(pl.multiple_of(tensor * quarter, quarter), quarter)
+    sources = (w_qkv, w_out.at[:, mine_columns], w_up, w_down)
+    wholes = (g_qkv, g_out, g_up, g_down)
+    lent = (1, 2)
 
     def piece(which, number):
-        source, whole = weights[which]
+        source, whole = sources[which], wholes[which]
         if which < 3:
             size = source.shape[0]
-            return whole.at[pl.ds(pl.multiple_of(number * size, size), size), :]
-        size = source.shape[1]
+            at = pl.ds(pl.multiple_of(number * size, size), size)
+            return whole.at[at, mine_columns] if which == 1 else whole.at[at, :]
         if narrow:
             return whole.at[number]
+        size = source.shape[1]
         return whole.at[:, pl.ds(pl.multiple_of(number * size, size), size)]
 
     def slot(buffer, number):
@@ -144,10 +151,168 @@
 
     own_tokens = pltpu.make_async_copy(slot(outgoing, me), slot(received, me), tok_ss.at[me])
 
+    def up_copy(which, source_high, src):
+        return remote(
+            src,
+            piece(which, source_high * 2 + low),
+            line_up.at[which, source_high],
+            line_rs.at[which, source_high],
+            above,
+        )
+
+    def down_copy(which, source_high, src):
+        return remote(
+            src,
+            piece(which, source_high * 2 + low),
+            line_down.at[which, source_high],
+            line_rs.at[which, source_high],
+            below,
+        )
+
+    def pair_copy(which, source_high, src):
+        return remote(
+            src,
+            piece(which, source_high * 2 + low),
+            pair_ss.at[which, source_high],
+            pair_rs.at[which, source_high],
+            pair,
+        )
+
+    has_above = high < half - 1
+    has_below = high > 0
+    in_lower = high < half // 2
+    lends_above = has_above & (high + 1 >= half // 2)
+    lends_below = has_below & (high - 1 < half // 2)
+    lender = jnp.where(in_lower, high + 1, high - 1)
+
+    owns = [
+        pltpu.make_async_copy(sources[which], piece(which, me), own_s.at[which])
+        for which in range(4)
+    ]
+
+    def send_own(which):
+        source = sources[which]
+
+        @pl.when(has_above)
+        def _():
+            up_copy(which, high, source).start()
+
+        @pl.when(has_below)
+        def _():
+            down_copy(which, high, source).start()
+
+        pair_copy(which, high, source).start()
+        owns[which].start()
+
+    def relay(which, back):
+        lower = high - back
+
+        @pl.when(lower >= 0)
+        def _():
+            src = piece(which, lower * 2 + low)
+            up_copy(which, lower, src).wait_recv()
+
+            @pl.when(has_above)
+            def _():
+                up_copy(which, lower, src).start()
+
+            if which in lent:
+
+                @pl.when(lower != lender)
+                def _():
+                    pair_copy(which, lower, src).start()
+
+            else:
+                pair_copy(which, lower, src).start()
+
+        upper = high + back
+
+        @pl.when(upper < half)
+        def _():
+            src = piece(which, upper * 2 + low)
+            down_copy(which, upper, src).wait_recv()
+
+            @pl.when(has_below)
+            def _():
+                down_copy(which, upper, src).start()
+
+            if which in lent:
+
+                @pl.when(upper != lender)
+                def _():
+                    pair_copy(which, upper, src).start()
+
+            else:
+                pair_copy(which, upper, src).start()
+
+    def pair_arrival(which, source_high):
+        other = piece(which, source_high * 2 + 1 - low)
+        return remote(
+            other, other, pair_ss.at[which, source_high], pair_rs.at[which, source_high], pair
+        )
+
+    def lend_copy(which, direction):
+        other = piece(which, high * 2 + 1 - low)
+        return remote(
+            other,
+            other,
+            lend_ss.at[which, direction],
+            lend_rs.at[which],
+            below if direction == 0 else above,
+        )
+
+    def lend(which):
+        pair_arrival(which, high).wait_recv()
+
+        @pl.when(lends_below)
+        def _():
+            lend_copy(which, 0).start()
+
+        @pl.when(lends_above)
+        def _():
+            lend_copy(which, 1).start()
+
+    def gathered(which):
+        owns[which].wait()
+        for source_high in range(half):
+            if which in lent:
+
+                @pl.when((high != source_high) & (lender != source_high))
+                def _():
+                    pair_arrival(which, source_high).wait_recv()
+
+            else:
+                pair_arrival(which, source_high).wait_recv()
+        if which in lent:
+            borrowed = piece(which, lender * 2 + 1 - low)
+            remote(
+                borrowed, borrowed, lend_ss.at[which, 0], lend_rs.at[which], above
+            ).wait_recv()
+
+    chunks = rows // CHUNK
+    parts = rows // TILE
+
+    def chunk_rows(chunk):
+        return pl.ds(pl.multiple_of(chunk * CHUNK, CHUNK), CHUNK)
+
+    def stream_copy(part):
+        at = pl.ds(part * TILE, TILE)
+        return remote(
+            stream.at[at, :], x.at[at, :], x_ss.at[part], x_rs.at[part], partner
+        )
+
+    out_swap = remote(
+        g_out.at[:, mine_columns], g_out.at[:, mine_columns], swap_s.at[0], swap_s.at[1], beside
+    )
+
+    @pl.when(second)
+    def _():
+        pl.semaphore_wait(go_sem, 1)
+
+    send_own(0)
+
     @pl.when(first)
     def _():
-        slots = outgoing.shape[0]
-
         @pl.loop(0, width // TILE)
         def _(tile):
             columns = pl.ds(pl.multiple_of(tile * TILE, TILE), TILE)
@@ -159,117 +324,15 @@
             token_copy(step).start()
         own_tokens.start()
 
-    @pl.when(second)
-    def _():
-        pl.semaphore_wait(go_sem, 1)
-
-    owns = []
-    for which in range(4):
-        own = pltpu.make_async_copy(weights[which][0], piece(which, me), own_s.at[which])
-        own.start()
-        owns.append(own)
-
-    def up_copy(which, source_high, src):
-        return remote(
-            src,
-            piece(which, source_high * 2 + low),
-            line_up.at[which, source_high],
-            line_rs.at[which, source_high],
-            above,
-        )
-
-    def down_copy(which, source_high, src):
-        return remote(
-            src,
-            piece(which, source_high * 2 + low),
-            line_down.at[which, source_high],
-            line_rs.at[which, source_high],
-            below,
-        )
-
-    def pair_copy(which, source_high, src):
-        return remote(
-            src,
-            piece(which, source_high * 2 + low),
-            pair_ss.at[which, source_high],
-            pair_rs.at[which, source_high],
-            pair,
-        )
-
-    has_above = high < half - 1
-    has_below = high > 0
-    for which in range(4):
-        source = weights[which][0]
-
-        @pl.when(has_above)
-        def _():
-            up_copy(which, high, source).start()
-
-        @pl.when(has_below)
-        def _():
-            down_copy(which, high, source).start()
-
-        pair_copy(which, high, source).start()
-
-    def relay(which, back):
-        lower = high - back
-
-        @pl.when(lower >= 0)
-        def _():
-            src = piece(which, lower * 2 + low)
-            arriving = up_copy(which, lower, src)
-            arriving.wait_recv()
-
-            @pl.when(has_above)
-            def _():
-                up_copy(which, lower, src).start()
-
-            pair_copy(which, lower, src).start()
-
-        upper = high + back
-
-        @pl.when(upper < half)
-        def _():
-            src = piece(which, upper * 2 + low)
-            arriving = down_copy(which, upper, src)
-            arriving.wait_recv()
-
-            @pl.when(has_below)
-            def _():
-                down_copy(which, upper, src).start()
-
-            pair_copy(which, upper, src).start()
-
+    send_own(1)
     for back in range(1, half):
-        for which in range(4):
-            relay(which, back)
-
-    @pl.when(first)
-    def _():
-        pl.semaphore_signal(
-            go_sem, inc=1, device_id=partner, device_id_type=pl.DeviceIdType.MESH
-        )
-
-    def gathered(which):
-        owns[which].wait()
-        for source_high in range(half):
-            other = piece(which, source_high * 2 + 1 - low)
-            remote(
-                other, other, pair_ss.at[which, source_high], pair_rs.at[which, source_high], pair
-            ).wait_recv()
-
-    chunks = rows // CHUNK
-
-    def chunk_rows(chunk):
-        return pl.ds(pl.multiple_of(chunk * CHUNK, CHUNK), CHUNK)
-
-    def stream_copy(part):
-        at = pl.ds(part * TILE, TILE)
-        return remote(
-            stream.at[at, :], x.at[at, :], x_ss.at[part], x_rs.at[part], partner
-        )
-
-    parts = rows // TILE
+        relay(0, back)
+    send_own(2)
+    for back in range(1, half):
+        relay(1, back)
+        if back == 1:
+            lend(1)
+    send_own(3)
 
     @pl.when(first)
     def _():
@@ -284,8 +347,13 @@
                 pick[...], received[:, columns], preferred_element_type=F32
             ).astype(BF)
 
-    for which in range(4):
-        gathered(which)
+    relay(2, 1)
+    lend(2)
+    gathered(0)
+    gathered(1)
+    out_swap.start()
+    for back in range(2, half):
+        relay(2, back)
 
     @pl.when(second)
     def _():
@@ -295,13 +363,14 @@
     @pl.loop(0, chunks)
     def _(chunk):
         at = chunk_rows(chunk)
-        normed[at, :] = normalised(x[at, :].astype(F32), gain_attn[...]).astype(BF)
+        normed[at, :] = normalised(x[at, :].astype(F32), gain_attn[...].astype(F32)).astype(BF)
 
     @pl.loop(0, merged.shape[1] // TILE)
     def _(tile):
         columns = pl.ds(pl.multiple_of(tile * TILE, TILE), TILE)
         merged[:, columns] = jnp.dot(normed[...], g_qkv[:, columns], preferred_element_type=F32)
 
+    turns = -(-(half - 1) // chunks)
     lanes = 2 * HEAD_DIM
     lane_of = lax.broadcasted_iota(jnp.int32, (CHUNK, lanes), 1)
     contract = (((1,), (1,)), ((), ()))
@@ -343,11 +412,21 @@
                 lane_of < HEAD_DIM, outs[0], outs[1]
             ).astype(BF)
         head_copy(chunk).start()
+        for turn in range(turns):
+            relay(3, chunk * turns + turn + 1)
+
+    @pl.when(first)
+    def _():
+        pl.semaphore_signal(
+            go_sem, inc=1, device_id=partner, device_id_type=pl.DeviceIdType.MESH
+        )
 
     @pl.loop(0, chunks)
     def _(chunk):
         head_copy(chunk).wait()
 
+    out_arrival = g_out.at[:, pl.ds(pl.multiple_of((1 - tensor) * quarter, quarter), quarter)]
+    remote(out_arrival, out_arrival, swap_s.at[0], swap_s.at[1], beside).wait_recv()
     mine_rows = pl.ds(pl.multiple_of(tensor * quarter, quarter), quarter)
     other_rows = pl.ds(pl.multiple_of((1 - tensor) * quarter, quarter), quarter)
 
@@ -363,19 +442,24 @@
     @pl.loop(0, chunks)
     def _(chunk):
         at = chunk_rows(chunk)
-        normed[at, :] = normalised(mid[at, :], gain_mlp[...]).astype(BF)
+        normed[at, :] = normalised(mid[at, :], gain_mlp[...].astype(F32)).astype(BF)
+
+    gathered(2)
 
     @pl.loop(0, hidden.shape[1] // TILE)
     def _(tile):
         columns = pl.ds(pl.multiple_of(tile * TILE, TILE), TILE)
         raised = (
-            jnp.dot(normed[...], g_up[:, columns], preferred_element_type=F32) + bias[:, columns]
+            jnp.dot(normed[...], g_up[:, columns], preferred_element_type=F32)
+            + bias[:, columns].astype(F32)
         )
         hidden[:, columns] = (raised * (1.0 + lax.erf(raised * (0.5**0.5))) * 0.5).astype(BF)
 
     def partial_copy(part):
         at = pl.ds(part * TILE, TILE)
         return remote(p_mine.at[at, :], p_other.at[at, :], p_ss.at[part], p_rs.at[part], beside)
+
+    gathered(3)
 
     for part in range(parts):
         at = pl.ds(part * TILE, TILE)
@@ -428,7 +512,7 @@
             centred = values - average
             scale = lax.rsqrt(jnp.mean(centred * centred, axis=-1, keepdims=True) + epsilon)
             piece_values = (
-                (stream[at, own_columns].astype(F32) - average) * scale * gain_final[:, own_columns]
+                (stream[at, own_columns].astype(F32) - average) * scale * gain_final[:, own_columns].astype(F32)
             )
             fin[pl.ds(chunk * per, per)] = piece_values.astype(BF).reshape(per, block, quarter)
 
@@ -444,8 +528,9 @@
             token_copy(step).wait_send()
         result.wait_recv()
 
+    out_swap.wait_send()
     for which in range(4):
-        source = weights[which][0]
+        source = sources[which]
         for back in range(half):
 
             @pl.when(has_above & (high - back >= 0))
@@ -456,7 +541,23 @@
             def _():
                 down_copy(which, high + back, source).wait_send()
 
-            pair_copy(which, back, source).wait_send()
+            if which in lent:
+
+                @pl.when(lender != back)
+                def _():
+                    pair_copy(which, back, source).wait_send()
+
+            else:
+                pair_copy(which, back, source).wait_send()
+        if which in lent:
+
+            @pl.when(lends_below)
+            def _():
+                lend_copy(which, 0).wait_send()
+
+            @pl.when(lends_above)
+            def _():
+                lend_copy(which, 1).wait_send()
 
 
 def local(
@@ -560,6 +661,9 @@
             dma((rows // TILE,)),
             dma((rows // TILE,)),
             dma((2,)),
+            dma((4, 2)),
+            dma((4,)),
+            dma((2,)),
             pltpu.SemaphoreType.REGULAR,
         ],
         compiler_params=pltpu.CompilerParams(
@@ -570,10 +674,10 @@
         select,
         pick,
         mask,
-        up_bias[0].astype(F32)[None],
-        attn_gain[0].astype(F32)[None],
-        mlp_gain[0].astype(F32)[None],
-        final_gain.astype(F32)[None],
+        up_bias,
+        attn_gain,
+        mlp_gain,
+        final_gain[None],
         w_qkv,
         w_out,
         w_up,

time: 225 us -> 194 us (0.86)
  Pallas kernels: 210 us -> 183 us
  other arithmetic: 11.7 us -> 6.62 us
    pallas_call x1, Pallas kernels: 210 us -> 183 us  [local(): pl.pallas_call(functools.partial(encoder, groups, cap_rows), out_shape=ja...]
    convert_element_type x3 -> x0, other arithmetic: 3.87 us -> none  [the longest x1 1.31 us: local(): up_bias[0].astype(F32)[None]]
where the time goes in v2:
time: 194 us
  Pallas kernels  183 us (94%)
  other arithmetic  6.62 us (3%)
  local copies, waits for them, and re-layouts  3.66 us (2%)
    pallas_call x1, Pallas kernels, local(): pl.pallas_call(functools.partial(encoder, groups, cap_rows), out_shape=ja...  183 us

profile of v2, /device:TPU:0, one launch (start us, length us, event | category | flops | bytes accessed | tf_op | source)
XLA Modules:
  0.0 193.6 jit_solution(1584932807188726543)
XLA Ops:
  0.0 0.8 select_reduce_fusion
  0.8 0.7 dynamic_slice.6
  1.6 0.2 convert_reduce_fusion
  1.7 0.1 dynamic-slice_multiply_fusion
  1.8 0.8 select_reduce_fusion.2
  2.7 0.1 broadcast_compare_fusion.1
  2.7 0.1 broadcast_in_dim.30
  2.8 0.1 tile.18
  2.9 1.3 broadcast_in_dim.66.gain_final
  4.2 0.1 broadcast_in_dim.31
  4.3 0.1 broadcast_in_dim.32
  4.4 0.1 iota_add_fusion
  4.4 0.1 add.82
  4.5 0.1 iota_add_fusion.1
  4.6 0.1 add.79
  4.7 0.1 broadcast_compare_fusion
  4.8 0.7 and_select_fusion.mask
  5.5 0.0 copy-done
  5.5 0.2 copy.15
  5.7 0.9 copy.16.w_qkv
  6.7 0.9 fusion.select
  7.6 1.0 fusion.1.pick
  8.6 183.3 %shard_map.109 = bf16[16,16,512]{2,1,0:T(8,128)(2,1)} custom-call(bf16[512,1024]{1,0:T(8,128)(2,1)} %bitcast.6, bf16[512,512]{1,0:T(8,128)(2,1)} %fusion.select, bf16[512,512]{1,0:T(8,128)(2,1)} %fusion.1.pick, f32[4,128,128]{2,1,0:T(8,128)} %and_select_fusion.mask, bf16[1,2048]{1,0:T(2,128)(2,1)} %bias.1, bf16[1,1024]{1,0:T(2,128)(2,1)} %gain_attn.1, ...), custom_call_target="tpu_custom_call" | custom-call | tf_op jit(solution)/shard_map/pallas_call | solution.py:626
  191.9 1.8 broadcast_select_fusion
  (8 shorter events, 0.0 us)
Async XLA Ops:
  0.0 5.5 %copy-start = (bf16[1,128,3,512]{3,1,2,0:T(8,128)(2,1)S(1)}, bf16[1,128,3,512]{3,1,2,0:T(8,128)(2,1)}, u32[]{:S(2)}) copy-start(bf16[1,128,3,512]{3,1,2,0:T(8,128)(2,1)} %param.14) | copy-start | bytes 1179652

commit v3 on v2

--- a/solution.py
+++ b/solution.py
@@ -118,7 +118,7 @@
     mine_columns = pl.ds(pl.multiple_of(tensor * quarter, quarter), quarter)
     sources = (w_qkv, w_out.at[:, mine_columns], w_up, w_down)
     wholes = (g_qkv, g_out, g_up, g_down)
-    lent = (1, 2)
+    lent = (0, 1)
 
     def piece(which, number):
         source, whole = sources[which], wholes[which]
@@ -327,10 +327,12 @@
     send_own(1)
     for back in range(1, half):
         relay(0, back)
+        if back == 1 and 0 in lent:
+            lend(0)
     send_own(2)
     for back in range(1, half):
         relay(1, back)
-        if back == 1:
+        if back == 1 and 1 in lent:
             lend(1)
     send_own(3)
 
@@ -348,7 +350,8 @@
             ).astype(BF)
 
     relay(2, 1)
-    lend(2)
+    if 2 in lent:
+        lend(2)
     gathered(0)
     gathered(1)
     out_swap.start()
@@ -455,44 +458,60 @@
         )
         hidden[:, columns] = (raised * (1.0 + lax.erf(raised * (0.5**0.5))) * 0.5).astype(BF)
 
-    def partial_copy(part):
-        at = pl.ds(part * TILE, TILE)
-        return remote(p_mine.at[at, :], p_other.at[at, :], p_ss.at[part], p_rs.at[part], beside)
-
-    gathered(3)
-
-    for part in range(parts):
-        at = pl.ds(part * TILE, TILE)
-
-        @pl.loop(0, width // TILE)
-        def _(tile):
-            columns = pl.ds(pl.multiple_of(tile * TILE, TILE), TILE)
-            if narrow:
-                count = TILE // g_down.shape[2]
-                product = jnp.concatenate(
-                    [
-                        jnp.dot(
-                            hidden[at, :], g_down[tile * count + i], preferred_element_type=F32
-                        )
-                        for i in range(count)
-                    ],
-                    axis=1,
-                )
-            else:
-                product = jnp.dot(hidden[at, :], g_down[:, columns], preferred_element_type=F32)
-            p_mine[at, columns] = product.astype(BF)
-
-        partial_copy(part).start()
-
-    for part in range(parts):
-        at = pl.ds(part * TILE, TILE)
-        partial_copy(part).wait()
-        stream[at, :] = (
-            mid[at, :] + (p_mine[at, :].astype(F32) + p_other[at, :].astype(F32))
-        ).astype(BF)
-
-        @pl.when(first)
-        def _():
+    size_down = w_down.shape[1]
+
+    def partial_copy(number):
+        return remote(
+            p_mine.at[number], p_other.at[number], p_ss.at[number], p_rs.at[number], beside
+        )
+
+    def partial(number):
+        if narrow:
+            columns_of = g_down[number]
+        else:
+            columns_of = g_down[:, pl.ds(pl.multiple_of(number * size_down, size_down), size_down)]
+        p_mine[number] = jnp.dot(hidden[...], columns_of, preferred_element_type=F32).astype(BF)
+        partial_copy(number).start()
+
+    owns[3].wait()
+
+    @pl.loop(0, half)
+    def _(source_high):
+        partial(source_high * 2 + low)
+
+    @pl.loop(0, half)
+    def _(step):
+        source_high = jnp.where(in_lower, high + step, high - step + half) % half
+        pair_arrival(3, source_high).wait_recv()
+        partial(source_high * 2 + 1 - low)
+
+    if narrow:
+        joined = TILE // size_down
+        tiles = [
+            (slice(t * TILE, (t + 1) * TILE), [t * joined + i for i in range(joined)])
+            for t in range(width // TILE)
+        ]
+    else:
+        tiles = [
+            (slice(t * size_down, (t + 1) * size_down), [t]) for t in range(width // size_down)
+        ]
+    for number in range(groups):
+        partial_copy(number).wait()
+
+    @pl.loop(0, parts)
+    def _(part):
+        at = pl.ds(pl.multiple_of(part * TILE, TILE), TILE)
+        for columns, numbers in tiles:
+            added = [
+                p_mine[number, at, :].astype(F32) + p_other[number, at, :].astype(F32)
+                for number in numbers
+            ]
+            added = added[0] if len(added) == 1 else jnp.concatenate(added, axis=1)
+            stream[at, columns] = (mid[at, columns] + added).astype(BF)
+
+    @pl.when(first)
+    def _():
+        for part in range(parts):
             stream_copy(part).start()
 
     result = remote(
@@ -642,8 +661,8 @@
             pltpu.VMEM((rows, quarter), BF),
             pltpu.VMEM((rows, width), F32),
             pltpu.VMEM((rows, units), BF),
-            pltpu.VMEM((rows, width), BF),
-            pltpu.VMEM((rows, width), BF),
+            pltpu.VMEM((groups, rows, down_columns), BF),
+            pltpu.VMEM((groups, rows, down_columns), BF),
             pltpu.VMEM((rows, width), BF),
             pltpu.VMEM((images_dev, block, quarter), BF),
             dma((groups,)),
@@ -656,8 +675,8 @@
             dma((4, half)),
             dma((rows // CHUNK,)),
             dma((rows // CHUNK,)),
-            dma((rows // TILE,)),
-            dma((rows // TILE,)),
+            dma((groups,)),
+            dma((groups,)),
             dma((rows // TILE,)),
             dma((rows // TILE,)),
             dma((2,)),

time: 194 us -> 182 us (0.938)
  Pallas kernels: 183 us -> 171 us
    pallas_call x1, Pallas kernels: 183 us -> 171 us  [local(): pl.pallas_call(functools.partial(encoder, groups, cap_rows), out_shape=ja...]
where the time goes in v3:
time: 182 us; the launch traced here: 181 us
  Pallas kernels  171 us (94%)
  other arithmetic  6.62 us (4%)
  local copies, waits for them, and re-layouts  3.66 us (2%)
    pallas_call x1, Pallas kernels, local(): pl.pallas_call(functools.partial(encoder, groups, cap_rows), out_shape=ja...  171 us

profile of v3, /device:TPU:0, one launch (start us, length us, event | category | flops | bytes accessed | tf_op | source)
XLA Modules:
  0.0 181.4 jit_solution(1845725742302883741)
XLA Ops:
  0.0 0.8 select_reduce_fusion
  0.8 0.7 dynamic_slice.6
  1.6 0.2 convert_reduce_fusion
  1.7 0.1 dynamic-slice_multiply_fusion
  1.8 0.8 select_reduce_fusion.2
  2.7 0.1 broadcast_compare_fusion.1
  2.7 0.1 broadcast_in_dim.30
  2.8 0.1 tile.18
  2.9 1.3 broadcast_in_dim.66.gain_final
  4.2 0.1 broadcast_in_dim.31
  4.3 0.1 broadcast_in_dim.32
  4.4 0.1 iota_add_fusion
  4.4 0.1 add.82
  4.5 0.1 iota_add_fusion.1
  4.6 0.1 add.79
  4.7 0.1 broadcast_compare_fusion
  4.8 0.7 and_select_fusion.mask
  5.5 0.0 copy-done
  5.5 0.2 copy.15
  5.7 0.9 copy.16.w_qkv
  6.7 0.9 fusion.select
  7.6 1.0 fusion.1.pick
  8.6 171.1 %shard_map.109 = bf16[16,16,512]{2,1,0:T(8,128)(2,1)} custom-call(bf16[512,1024]{1,0:T(8,128)(2,1)} %bitcast.6, bf16[512,512]{1,0:T(8,128)(2,1)} %fusion.select, bf16[512,512]{1,0:T(8,128)(2,1)} %fusion.1.pick, f32[4,128,128]{2,1,0:T(8,128)} %and_select_fusion.mask, bf16[1,2048]{1,0:T(2,128)(2,1)} %bias.1, bf16[1,1024]{1,0:T(2,128)(2,1)} %gain_attn.1, ...), custom_call_target="tpu_custom_call" | custom-call | tf_op jit(solution)/shard_map/pallas_call | solution.py:645
  179.6 1.8 broadcast_select_fusion
  (8 shorter events, 0.0 us)
Async XLA Ops:
  0.0 5.5 %copy-start = (bf16[1,128,3,512]{3,1,2,0:T(8,128)(2,1)S(1)}, bf16[1,128,3,512]{3,1,2,0:T(8,128)(2,1)}, u32[]{:S(2)}) copy-start(bf16[1,128,3,512]{3,1,2,0:T(8,128)(2,1)} %param.14) | copy-start | bytes 1179652

commit v4 on v3

--- a/solution.py
+++ b/solution.py
@@ -305,11 +305,11 @@
         g_out.at[:, mine_columns], g_out.at[:, mine_columns], swap_s.at[0], swap_s.at[1], beside
     )
 
+    send_own(0)
+
     @pl.when(second)
     def _():
         pl.semaphore_wait(go_sem, 1)
-
-    send_own(0)
 
     @pl.when(first)
     def _():

time: 182 us -> 174 us (0.956)
  Pallas kernels: 171 us -> 164 us
    pallas_call x1, Pallas kernels: 171 us -> 164 us  [local(): pl.pallas_call(functools.partial(encoder, groups, cap_rows), out_shape=ja...]
where the time goes in v4:
time: 174 us
  Pallas kernels  164 us (94%)
  other arithmetic  6.62 us (4%)
  local copies, waits for them, and re-layouts  3.66 us (2%)
    pallas_call x1, Pallas kernels, local(): pl.pallas_call(functools.partial(encoder, groups, cap_rows), out_shape=ja...  164 us

profile of v4, /device:TPU:0, one launch (start us, length us, event | category | flops | bytes accessed | tf_op | source)
XLA Modules:
  0.0 174.2 jit_solution(17682962456558510888)
XLA Ops:
  0.0 0.8 select_reduce_fusion
  0.8 0.7 dynamic_slice.6
  1.6 0.2 convert_reduce_fusion
  1.7 0.1 dynamic-slice_multiply_fusion
  1.8 0.8 select_reduce_fusion.2
  2.7 0.1 broadcast_compare_fusion.1
  2.7 0.1 broadcast_in_dim.30
  2.8 0.1 tile.18
  2.9 1.3 broadcast_in_dim.66.gain_final
  4.2 0.1 broadcast_in_dim.31
  4.3 0.1 broadcast_in_dim.32
  4.4 0.1 iota_add_fusion
  4.4 0.1 add.82
  4.5 0.1 iota_add_fusion.1
  4.6 0.1 add.79
  4.7 0.1 broadcast_compare_fusion
  4.8 0.7 and_select_fusion.mask
  5.5 0.0 copy-done
  5.5 0.2 copy.15
  5.7 0.9 copy.16.w_qkv
  6.7 0.9 fusion.select
  7.6 1.0 fusion.1.pick
  8.6 163.9 %shard_map.109 = bf16[16,16,512]{2,1,0:T(8,128)(2,1)} custom-call(bf16[512,1024]{1,0:T(8,128)(2,1)} %bitcast.6, bf16[512,512]{1,0:T(8,128)(2,1)} %fusion.select, bf16[512,512]{1,0:T(8,128)(2,1)} %fusion.1.pick, f32[4,128,128]{2,1,0:T(8,128)} %and_select_fusion.mask, bf16[1,2048]{1,0:T(2,128)(2,1)} %bias.1, bf16[1,1024]{1,0:T(2,128)(2,1)} %gain_attn.1, ...), custom_call_target="tpu_custom_call" | custom-call | tf_op jit(solution)/shard_map/pallas_call | solution.py:645
  172.4 1.8 %broadcast_select_fusion = bf16[16,16,512]{2,1,0:T(8,128)(2,1)} fusion(bf16[16,16,512]{2,1,0:T(8,128)(2,1)} %shard_map.109, pred[16,16]{1,0:T(8,128)(4,1)S(1)} %broadcast_compare_fusion.1), kind=kLoop, calls=%fused_computation.5 | loop fusion | flops 131072 | bytes 524544 | tf_op jit(solution)/shard_map/jit(_where)/select_n | solution.py:707
  (8 shorter events, 0.0 us)
Async XLA Ops:
  0.0 5.5 %copy-start = (bf16[1,128,3,512]{3,1,2,0:T(8,128)(2,1)S(1)}, bf16[1,128,3,512]{3,1,2,0:T(8,128)(2,1)}, u32[]{:S(2)}) copy-start(bf16[1,128,3,512]{3,1,2,0:T(8,128)(2,1)} %param.14) | copy-start | bytes 1179652
